TPU v7x, 128 devices: a whole 4x4x4 slice. The times are simulated.
128 devices in a mesh: seq: 16 (over x, y), exp: 8 (over z, core).
Axes of the slice: x: 4, y: 4, z: 4, core: 2. Of those that a mesh axis runs over, the one named last changes fastest.
Arguments:
- upstream: bfloat16 [8192, 6144], P(('seq', 'exp')), may hold values from -6 to 6
- out_weight: bfloat16 [4096, 6144], P('exp'), may hold values from -0.078125 to 0.078125
- queries: bfloat16 [8192, 4096], P('seq', 'exp'), may hold values from -6 to 6
- keys: bfloat16 [8192, 4096], P('seq', 'exp'), may hold values from -6 to 6
- values: bfloat16 [8192, 4096], P('seq', 'exp'), may hold values from -6 to 6
- log_decay: float32 [32, 8192], P('exp', 'seq'), may hold values from -0.8 to 0, as said below
- expert_ids: int32 [8192, 2], P(('seq', 'exp')), may hold values from 0 to 15, all different within a row; in each aligned block of 64 rows (0 to 63, 64 to 127, ...) at most 9 rows name the same one
- gate_probs: float32 [8192, 2], P(('seq', 'exp')), may hold values from 0.05 to 0.95
- activations: bfloat16 [16, 4608, 1152], P('exp', 'seq'), may hold values from -1.5 to 1.5
Outputs:
- d_queries: bfloat16 [8192, 4096], P('seq', 'exp')
- d_keys: bfloat16 [8192, 4096], P('seq', 'exp')
- d_values: bfloat16 [8192, 4096], P('seq', 'exp')
- d_down: bfloat16 [16, 4608, 6144], P('exp', 'seq')
Inputs may be any that keep to these rules, and one draw needn't show every extreme that they name: `expert_ids`: each row names two different experts. In every block of 64 rows no expert is named more than 9 times, and in every draw some block names some expert exactly 9 times. `log_decay`: negative at every position.
All inputs are finite; a program needn't handle non-finite values.
Results may differ from a plain program's by a relative error of at most 0.005.
Values may be sent and summed in bfloat16 or wider, within the bound.
A program may use at most 192 MiB of HBM per device.

v0:
```python
import math
import jax
import jax.numpy as jnp
from jax import lax
from jax.sharding import PartitionSpec as P

HEAD = 128
EXPERTS = 16
HIGH = lax.Precision.HIGHEST


def prefix(value, axis, join, neutral, backward):
    count, mine = (lax.axis_size(axis), lax.axis_index(axis))
    pieces = jax.tree.map(lambda part: lax.all_gather(part, axis), value)
    if backward:
        pieces = jax.tree.map(lambda part: part[::-1], pieces)
        mine = count - 1 - mine
    so_far = jax.tree.map(
        lambda part, zero: jnp.full_like(part, 0) + jnp.asarray(zero, part.dtype), value, neutral
    )

    def hop(position, so_far):
        longer = join(so_far, jax.tree.map(lambda part: part[position], pieces))
        return jax.tree.map(lambda new, old: jnp.where(position < mine, new, old), longer, so_far)

    return lax.fori_loop(0, count - 1, hop, so_far)


def block_terms(
    raw_query,
    raw_key,
    raw_value,
    raw_grad,
    query_heads,
    key_heads,
    value_heads,
    grad_heads,
    cumulative,
    lead,
    tail,
    state_in,
    adjoint_in,
):
    length = cumulative.shape[1]
    position = jnp.arange(length)
    lower = position[:, None] >= position[None, :]
    spread = cumulative[:, :, None] - cumulative[:, None, :]
    weights = jnp.where(lower[None], jnp.exp(jnp.minimum(spread, 0.0)), 0.0)
    mixed = (
        jnp.einsum("thf,shf->hts", raw_grad, raw_value, preferred_element_type=jnp.float32)
        * weights
    )
    paired = (
        jnp.einsum("the,she->hts", raw_query, raw_key, preferred_element_type=jnp.float32) * weights
    )
    d_query = jnp.einsum("hts,she->the", mixed, key_heads, precision=HIGH) + lead * jnp.einsum(
        "thf,hef->the", grad_heads, state_in, precision=HIGH
    )
    d_key = jnp.einsum("hts,the->she", mixed, query_heads, precision=HIGH) + tail * jnp.einsum(
        "shf,hef->she", value_heads, adjoint_in, precision=HIGH
    )
    d_value = jnp.einsum("hts,thf->shf", paired, grad_heads, precision=HIGH) + tail * jnp.einsum(
        "she,hef->shf", key_heads, adjoint_in, precision=HIGH
    )
    return (d_query, d_key, d_value)


def forward_join(earlier, later):
    return (earlier[0] * later[0], later[0][:, None, None] * earlier[1] + later[1])


def reverse_join(earlier, later):
    return (earlier[0] * later[0], later[1] + later[0][:, None, None] * earlier[1])


def shards(
    upstream, out_weight, queries, keys, values, log_decay, expert_ids, gate_probs, activations
):
    seq_count = lax.axis_size("seq")
    exp_count = lax.axis_size("exp")
    rows_here = queries.shape[0]
    heads_here = queries.shape[1] // HEAD
    scale = 1.0 / math.sqrt(HEAD * rows_here * seq_count)
    most = activations.shape[2] // (seq_count * exp_count)
    model_width = upstream.shape[1]
    grad_out = jnp.einsum(
        "td,fd->tf",
        lax.all_gather(upstream, "exp", axis=0, tiled=True),
        out_weight,
        preferred_element_type=jnp.float32,
    ).astype(jnp.bfloat16)
    flat_experts = expert_ids.reshape(-1)
    onehot = (flat_experts[:, None] == jnp.arange(EXPERTS, dtype=jnp.int32)[None, :]).astype(
        jnp.int32
    )
    earlier = jnp.cumsum(onehot, axis=0) - onehot
    rank = jnp.sum(earlier * onehot, axis=1)
    slot = flat_experts * most + rank
    routed = (
        (gate_probs[:, :, None] * upstream[:, None, :].astype(jnp.float32))
        .astype(jnp.bfloat16)
        .reshape(-1, model_width)
    )
    select = (jnp.arange(EXPERTS * most, dtype=jnp.int32)[:, None] == slot[None, :]).astype(
        jnp.bfloat16
    )
    outgoing = (
        jnp.dot(select, routed, preferred_element_type=jnp.float32)
        .astype(jnp.bfloat16)
        .reshape(EXPERTS, most, model_width)
    )
    incoming = lax.all_to_all(outgoing, "exp", split_axis=0, concat_axis=1, tiled=True)

    def split_raw(block):
        return block.reshape(rows_here, heads_here, HEAD)

    raw_query = split_raw(queries)
    raw_key = split_raw(keys)
    raw_value = split_raw(values)
    raw_grad = split_raw(grad_out)
    query_heads = raw_query.astype(jnp.float32)
    key_heads = raw_key.astype(jnp.float32)
    value_heads = raw_value.astype(jnp.float32)
    grad_heads = raw_grad.astype(jnp.float32)
    cumulative = jnp.cumsum(log_decay, axis=1)
    totals = cumulative[:, -1]
    lead = jnp.exp(cumulative).T[:, :, None]
    tail = jnp.exp(cumulative[:, -1:] - cumulative).T[:, :, None]
    kv_sum = jnp.einsum("she,shf->hef", key_heads * tail, value_heads, precision=HIGH)
    qo_sum = jnp.einsum("the,thf->hef", query_heads * lead, grad_heads, precision=HIGH)
    head_decay = jnp.exp(totals)
    identity_pair = (
        jnp.ones((heads_here,), jnp.float32),
        jnp.zeros((heads_here, HEAD, HEAD), jnp.float32),
    )
    state_in = prefix((head_decay, kv_sum), "seq", forward_join, identity_pair, False)[1]
    adjoint_in = prefix((head_decay, qo_sum), "seq", reverse_join, identity_pair, True)[1]
    d_query, d_key, d_value = block_terms(
        raw_query,
        raw_key,
        raw_value,
        raw_grad,
        query_heads,
        key_heads,
        value_heads,
        grad_heads,
        cumulative,
        lead,
        tail,
        state_in,
        adjoint_in,
    )
    width = heads_here * HEAD
    d_queries = (scale * d_query).reshape(rows_here, width).astype(jnp.bfloat16)
    d_keys = (scale * d_key).reshape(rows_here, width).astype(jnp.bfloat16)
    d_values = (scale * d_value).reshape(rows_here, width).astype(jnp.bfloat16)
    gathered = lax.all_gather(incoming, "seq", axis=1, tiled=True)
    d_down = jnp.einsum("ehs,esd->ehd", activations, gathered, preferred_element_type=jnp.float32)
    return (d_queries, d_keys, d_values, d_down.astype(jnp.bfloat16))


def solution(mesh):
    return jax.shard_map(
        shards,
        mesh=mesh,
        in_specs=(
            P(("seq", "exp"), None),
            P("exp", None),
            P("seq", "exp"),
            P("seq", "exp"),
            P("seq", "exp"),
            P("exp", "seq"),
            P(("seq", "exp"), None),
            P(("seq", "exp"), None),
            P("exp", "seq", None),
        ),
        out_specs=(P("seq", "exp"), P("seq", "exp"), P("seq", "exp"), P("exp", "seq", None)),
        check_vma=False,
    )
```

profile of v0, /device:TPU:1, one launch (start us, length us, event | category | flops | bytes accessed | tf_op | source)
XLA Modules:
  0.0 360.2 jit_solution(13961593589067682039)
XLA Ops:
  8.7 1.2 reduce-window.6
  10.5 1.3 copy.50
  11.8 2.5 fusion.47
  14.5 1.3 copy.54
  15.7 38.8 %all-gather.8.cloned.1.call-done = bf16[512,6144]{1,0:T(8,128)(2,1)} async-done(((bf16[64,6144]{1,0:T(8,128)(2,1)}), bf16[512,6144]{1,0:T(8,128)(2,1)}) %all-gather.8.cloned.1.call-update) | async-done | bytes 6291472 | tf_op jit(solution)/shard_map/all_gather | solution.py:88
  54.5 8.0 %convolution_convert_fusion.2 = bf16[512,512]{0,1:T(8,128)(2,1)S(1)} fusion(bf16[512,6144]{1,0:T(8,128)(2,1)} %all-gather.8.cloned.1.call-done, bf16[512,6144]{1,0:T(8,128)(2,1)} %param.14), kind=kOutput, calls=%fused_computation.44 | convolution fusion | flops 3221487616 | bytes 13107200 | tf_op jit(solution)/shard_map/td,fd->tf/dot_general | solution.py:86
  63.4 1.4 fusion.44
  65.1 3.2 mul.145
  68.3 5.1 %mul.146 = f32[128,6144]{1,0:T(8,128)} reshape(f32[64,2,6144]{2,1,0:T(2,128)} %mul.145) | data formatting | bytes 6291456 | tf_op jit(solution)/shard_map/mul | solution.py:100
  74.1 2.6 convolution_convert_fusion.1
  76.7 2.1 reshape.116
  78.8 41.6 %all_to_all.18 = bf16[16,9,6144]{2,1,0:T(8,128)(2,1)S(1)} all-to-all(bf16[16,9,6144]{2,1,0:T(8,128)(2,1)} %reshape.116), channel_id=1, replica_groups=mesh['seq'=16,'exp'=8] {'exp'}, dimensions={0} | all-to-all | bytes 3538944 | tf_op jit(solution)/shard_map/all_to_all | solution.py:112
  120.4 1.9 copy.63
  122.4 1.8 copy.64
  125.8 33.6 %all-reduce = f32[64]{0:T(128)S(1)} all-reduce(f32[64]{0:T(128)S(1)} %bitcast_dynamic-update-slice_fusion), channel_id=2, replica_groups=mesh['seq'=16,'exp'=8] {'seq'}, use_global_device_ids=true, to_apply=%add | all-reduce | flops 64 | bytes 512
  160.3 2.7 fusion.64
  163.0 16.6 %while.28 = (s32[]{:T(128)}, f32[4,128,128]{2,1,0:T(8,128)S(1)}, s32[]{:T(128)}, f32[16,4]{1,0:T(8,128)S(1)}, f32[16,4,128,128]{3,2,1,0:T(8,128)}, /*index=5*/s32[]{:T(128)}, s32[]{:T(128)}) while((s32[]{:T(128)}, f32[4,128,128]{2,1,0:T(8,128)S(1)}, s32[]{:T(128)}, f32[16,4]{1,0:T(8,128)S(1)}, f32[16,4,128,128]{3,2,1,0:T(8,128)}, ...), condition=%wide.region_3.4_spmd.clone, body=%wide.region_2.3_spmd.clone.sunk | while | flops 262148 | bytes 786585 | solution.py:26
  171.8 1.1 fusion.86
  172.9 1.1 fusion.86
  174.1 1.1 fusion.86
  175.2 1.1 fusion.86
  176.3 1.1 fusion.86
  179.6 1.8 fusion.52
  181.5 3.5 fusion.23
  184.9 1.4 fusion.41
  186.3 2.1 copy.65
  188.5 6.1 %fusion.29 = f32[512,4,128]{0,2,1:T(8,128)} fusion(bf16[512,4,128]{0,2,1:T(8,128)(2,1)S(1)} %bitcast.133, f32[4,512,512]{2,1,0:T(8,128)} %fusion.64, f32[4,512]{1,0:T(4,128)S(1)} %bitcast.141, pred[512,512]{1,0:T(8,128)(4,1)} %iota_compare_fusion), kind=kOutput, calls=%fused_computation.31 | convolution fusion | flops 1614807040 | bytes 6037504 | tf_op jit(solution)/shard_map/hts,thf->shf/dot_general | solution.py:62
  194.6 3.9 %fusion.26 = f32[512,4,128]{0,2,1:T(8,128)} fusion(bf16[512,4,128]{0,2,1:T(8,128)(2,1)S(1)} %bitcast.125, f32[4,512,512]{2,1,0:T(8,128)S(1)} %copy-done.8, f32[4,512]{1,0:T(4,128)S(1)} %bitcast.142, pred[512,512]{1,0:T(8,128)(4,1)S(1)} %copy-done.12), kind=kOutput, calls=%fused_computation.30 | convolution fusion | flops 1614807040 | bytes 6037504 | tf_op jit(solution)/shard_map/hts,the->she/dot_general | solution.py:59
  198.5 4.7 %rev.6 = f32[16,4,128,128]{3,2,1,0:T(8,128)} reverse(f32[16,4,128,128]{3,2,1,0:T(8,128)} %bitcast.134), dimensions={0} | reverse | bytes 8388608 | tf_op jit(solution)/shard_map/rev | solution.py:16
  203.2 16.8 %while.29 = (s32[]{:T(128)}, f32[4,128,128]{2,1,0:T(8,128)S(1)}, s32[]{:T(128)}, f32[16,4,128,128]{3,2,1,0:T(8,128)}, f32[16,4]{1,0:T(8,128)S(1)}, /*index=5*/s32[]{:T(128)}, s32[]{:T(128)}) while((s32[]{:T(128)}, f32[4,128,128]{2,1,0:T(8,128)S(1)}, s32[]{:T(128)}, f32[16,4,128,128]{3,2,1,0:T(8,128)}, f32[16,4]{1,0:T(8,128)S(1)}, ...), condition=%wide.region_5.6_spmd.clone, body=%wide.region_4.5_spmd.clone.sunk | while | flops 262148 | bytes 786585 | solution.py:26
  203.2 1.1 fusion.87
  204.4 1.1 fusion.87
  205.5 1.1 fusion.87
  206.6 1.1 fusion.87
  207.7 1.1 fusion.87
  208.8 1.1 fusion.87
  209.8 1.1 fusion.87
  210.9 1.1 fusion.87
  212.0 1.1 fusion.87
  214.2 1.1 fusion.87
  215.3 1.1 fusion.87
  216.5 1.1 fusion.87
  217.7 1.1 fusion.87
  218.8 1.1 fusion.87
  220.0 1.9 fusion.43
  222.9 1.8 fusion.42
  225.7 107.3 %all-gather.10.cloned.1.call-done = bf16[2,1152,6144]{2,1,0:T(8,128)(2,1)} async-done(((bf16[2,72,6144]{2,1,0:T(8,128)(2,1)}), bf16[2,1152,6144]{2,1,0:T(8,128)(2,1)}) %all-gather.10.cloned.1.call-update) | async-done | bytes 28311568 | tf_op jit(solution)/shard_map/all_gather | solution.py:157
  333.0 20.7 %fusion.2 = bf16[2,288,6144]{2,1,0:T(8,128)(2,1)} fusion(bf16[2,288,1152]{2,1,0:T(8,128)(2,1)S(1)} %copy-done, bf16[2,1152,6144]{2,1,0:T(8,128)(2,1)} %all-gather.10.cloned.1.call-done), kind=kOutput, calls=%fused_computation.7 | convolution fusion | flops 8157265920 | bytes 36716544 | tf_op jit(solution)/shard_map/ehs,esd->ehd/dot_general | solution.py:158
  (109 shorter events, 19.7 us)
Async XLA Ops:
  7.2 325.9 %copy-start = (bf16[2,288,1152]{2,1,0:T(8,128)(2,1)S(1)}, bf16[2,288,1152]{2,1,0:T(8,128)(2,1)}, u32[]{:S(2)}) copy-start(bf16[2,288,1152]{2,1,0:T(8,128)(2,1)} %param.21) | copy-start | bytes 3981316
  7.2 47.4 %all-gather.8.cloned.1.call-start = ((), (), s32[]{:S(2)}) async-start(), calls=%async_computation.1 | async-start | bytes 7077888 | tf_op jit(solution)/shard_map/all_gather | solution.py:88
  7.9 155.1 %all-gather.12.cloned.1.call-start = ((), (), s32[]{:S(2)}) async-start(), calls=%async_computation.3 | async-start | bytes 4456448 | tf_op jit(solution)/shard_map/all_gather | solution.py:14
  11.7 2.7 copy-start.3
  14.4 184.1 %all-gather.14.cloned.1.call-start = ((), (), s32[]{:S(2)}) async-start(), calls=%async_computation.4 | async-start | bytes 4456448 | tf_op jit(solution)/shard_map/all_gather | solution.py:14
  15.7 46.9 %copy-start.1 = (bf16[512,512]{0,1:T(8,128)(2,1)}, bf16[512,512]{0,1:T(8,128)(2,1)S(1)}, u32[]{:S(2)}) copy-start(bf16[512,512]{0,1:T(8,128)(2,1)S(1)} %copy.54) | copy-start | bytes 1572868
  15.7 49.1 %copy-start.13 = (s32[64,2]{0,1:T(2,128)S(1)}, s32[64,2]{0,1:T(2,128)}, u32[]{:S(2)}) copy-start(s32[64,2]{0,1:T(2,128)} %param.19) | copy-start | bytes 1540
  15.7 49.3 %copy-start.9 = (bf16[64,6144]{1,0:T(8,128)(2,1)S(1)}, bf16[64,6144]{1,0:T(8,128)(2,1)}, u32[]{:S(2)}) copy-start(bf16[64,6144]{1,0:T(8,128)(2,1)} %param.13) | copy-start | bytes 2359300
  62.6 0.8 copy-start.5
  64.8 268.3 %all-gather.10.cloned.1.call-start = ((), (), s32[]{:S(2)}) async-start(), calls=%async_computation.2 | async-start | bytes 30081024 | tf_op jit(solution)/shard_map/all_gather | solution.py:157
  65.1 8.3 %copy-start.14 = (f32[64,2]{0,1:T(2,128)S(1)}, f32[64,2]{0,1:T(2,128)}, u32[]{:S(2)}) copy-start(f32[64,2]{0,1:T(2,128)} %param.20) | copy-start | bytes 1540
  120.4 3.8 %copy-start.15 = (u32[128]{0:T(128)S(1)}, u32[128]{0:T(128)}, u32[]{:S(2)}) copy-start(u32[128]{0:T(128)} %constant.76) | copy-start | bytes 1540
  120.4 39.9 %copy-start.2 = (bf16[512,512]{0,1:T(8,128)(2,1)S(1)}, bf16[512,512]{0,1:T(8,128)(2,1)}, u32[]{:S(2)}) copy-start(bf16[512,512]{0,1:T(8,128)(2,1)} %copy-done.1) | copy-start | bytes 1572868
  120.4 39.9 %copy-start.4 = (bf16[512,512]{0,1:T(8,128)(2,1)S(1)}, bf16[512,512]{0,1:T(8,128)(2,1)}, u32[]{:S(2)}) copy-start(bf16[512,512]{0,1:T(8,128)(2,1)} %copy-done.3) | copy-start | bytes 1572868
  160.3 19.3 %copy-start.6 = (bf16[512,512]{0,1:T(8,128)(2,1)S(1)}, bf16[512,512]{0,1:T(8,128)(2,1)}, u32[]{:S(2)}) copy-start(bf16[512,512]{0,1:T(8,128)(2,1)} %copy-done.5) | copy-start | bytes 1572868
  179.6 1.9 copy-start.11
  181.5 4.9 %copy-start.7 = (f32[4,512,512]{2,1,0:T(8,128)}, f32[4,512,512]{2,1,0:T(8,128)S(1)}, u32[]{:S(2)}) copy-start(f32[4,512,512]{2,1,0:T(8,128)S(1)} %fusion.52) | copy-start | bytes 12582916
  186.3 8.3 %copy-start.12 = (pred[512,512]{1,0:T(8,128)(4,1)S(1)}, pred[512,512]{1,0:T(8,128)(4,1)}, u32[]{:S(2)}) copy-start(pred[512,512]{1,0:T(8,128)(4,1)} %iota_compare_fusion) | copy-start | bytes 786436
  188.5 6.1 %copy-start.8 = (f32[4,512,512]{2,1,0:T(8,128)S(1)}, f32[4,512,512]{2,1,0:T(8,128)}, u32[]{:S(2)}) copy-start(f32[4,512,512]{2,1,0:T(8,128)} %copy-done.7) | copy-start | bytes 12582916
  203.2 19.7 %copy-start.10 = (bf16[512,512]{1,0:T(8,128)(2,1)S(1)}, bf16[512,512]{1,0:T(8,128)(2,1)}, u32[]{:S(2)}) copy-start(bf16[512,512]{1,0:T(8,128)(2,1)} %param.17) | copy-start | bytes 1572868
Sparse Core Ops, SparseCore 0:
  9.7 44.7 all-gather.7
  56.7 50.9 all-gather.11
  109.8 51.4 all-gather.13
  163.3 169.6 all-gather.9
where the time goes:
time: 362 us; the launch traced here: 360 us
  waiting for transfers between devices  147 us (41%)
  blocking collectives  75.2 us (21%)
  matrix products  58.3 us (16%)
  other arithmetic  34.9 us (10%)
  local copies, waits for them, and re-layouts  29.2 us (8%)
  between operations  14.7 us (4%)
    all_gather x1, waiting for transfers between devices, shards(): gathered = lax.all_gather(incoming, 'seq', axis=1, tiled=True)  107 us
    all_to_all x1, blocking collectives, shards(): lax.all_to_all(outgoing, 'exp', split_axis=0, concat_axis=1, tiled=True)  41.6 us
    all_gather x1, waiting for transfers between devices, shards(): lax.all_gather(upstream, 'exp', axis=0, tiled=True)  38.8 us
    unnamed x1, blocking collectives  33.6 us
    select_n x30, other arithmetic, hop(): jnp.where(position < mine, new, old)  32.1 us
    dot_general x1, matrix products, shards(): jnp.einsum('ehs,esd->ehd', activations, gathered, preferred_element_type=...  20.7 us
    unnamed x44, local copies, waits for them, and re-layouts  8.72 us
    mul x3, local copies, waits for them, and re-layouts, shards(): gate_probs[:, :, None] * upstream[:, None, :].astype(jnp.float32)  8.43 us
  transfers between devices with their start and end apart: 4, of which 2 were waited for; matrix products, arithmetic and copies ran while one was open for 28% of the time, Pallas kernels for 0%

commit v1 on v0

--- a/solution.py
+++ b/solution.py
@@ -154,7 +154,10 @@
     d_queries = (scale * d_query).reshape(rows_here, width).astype(jnp.bfloat16)
     d_keys = (scale * d_key).reshape(rows_here, width).astype(jnp.bfloat16)
     d_values = (scale * d_value).reshape(rows_here, width).astype(jnp.bfloat16)
-    gathered = lax.all_gather(incoming, "seq", axis=1, tiled=True)
+    size = lax.axis_size("seq")
+    parts = jnp.stack([incoming for _ in range(size)])
+    parts = lax.all_to_all(parts, "seq", split_axis=0, concat_axis=0)
+    gathered = jnp.concatenate(parts, axis=1)
     d_down = jnp.einsum("ehs,esd->ehd", activations, gathered, preferred_element_type=jnp.float32)
     return (d_queries, d_keys, d_values, d_down.astype(jnp.bfloat16))
 

time: 362 us -> 779 us (2.15)
  blocking collectives: 75.2 us -> 598 us
  waiting for transfers between devices: 147 us -> 0.74 us
  local copies, waits for them, and re-layouts: 29.2 us -> 55.8 us
    unnamed x1, blocking collectives: 33.6 us -> 536 us
    all_gather x1 -> x0, waiting for transfers between devices: 107 us -> none  [shards(): gathered = lax.all_gather(incoming, 'seq', axis=1, tiled=True)]
    all_gather x1, waiting for transfers between devices: 38.8 us -> 0.02 us  [shards(): lax.all_gather(upstream, 'exp', axis=0, tiled=True)]
    all_to_all x1, blocking collectives: 41.6 us -> 62.3 us  [shards(): lax.all_to_all(outgoing, 'exp', split_axis=0, concat_axis=1, tiled=True)]
    reshape x1 -> x2, local copies, waits for them, and re-layouts: 0.71 us -> 19.7 us  [the longest x1 19.7 us: shards(): gathered = jnp.concatenate(parts, axis=1)]
    another operation x0 -> x2, local copies, waits for them, and re-layouts: none -> 10.1 us  [shards(): parts = jnp.stack([incoming for _ in range(size)])]
  transfers between devices with their start and end apart: 4 -> 4, of which waited for: 2 -> 0; matrix products, arithmetic and copies ran while one was open for 28% -> 14% of each run, Pallas kernels for 0% -> 0%
where the time goes in v1:
time: 779 us; the launch traced here: 769 us
  blocking collectives  598 us (77%)
  matrix products  57.3 us (7%)
  local copies, waits for them, and re-layouts  55.8 us (7%)
  other arithmetic  34.5 us (4%)
  between operations  14.7 us (2%)
    unnamed x1, blocking collectives  536 us
    all_to_all x1, blocking collectives, shards(): lax.all_to_all(outgoing, 'exp', split_axis=0, concat_axis=1, tiled=True)  62.3 us
    select_n x30, other arithmetic, hop(): jnp.where(position < mine, new, old)  31.7 us
    dot_general x1, matrix products, shards(): jnp.einsum('ehs,esd->ehd', activations, gathered, preferred_element_type=...  20.9 us
    reshape x1, local copies, waits for them, and re-layouts, shards(): gathered = jnp.concatenate(parts, axis=1)  19.7 us
  transfers between devices with their start and end apart: 4, of which 0 were waited for; matrix products, arithmetic and copies ran while one was open for 14% of the time, Pallas kernels for 0%

profile of v1, /device:TPU:1, one launch (start us, length us, event | category | flops | bytes accessed | tf_op | source)
XLA Modules:
  0.0 769.5 jit_solution(17392569603945511714)
XLA Ops:
  9.7 4.3 mul.145
  14.1 5.1 mul.146
  19.6 2.6 convolution_convert_fusion.1
  22.2 2.1 reshape.125
  24.3 62.3 %all_to_all.20 = bf16[16,9,6144]{2,1,0:T(8,128)(2,1)S(1)} all-to-all(bf16[16,9,6144]{2,1,0:T(8,128)(2,1)} %reshape.125), channel_id=1, replica_groups=mesh['seq'=16,'exp'=8] {'exp'}, dimensions={0} | all-to-all | bytes 3538944 | tf_op jit(solution)/shard_map/all_to_all | solution.py:112
  86.6 1.9 copy.62
  89.0 9.6 %stack.5 = bf16[16,2,72,6144]{3,2,1,0:T(8,128)(2,1)} broadcast(bf16[2,72,6144]{2,1,0:T(8,128)(2,1)S(1)} %copy.63), dimensions={1,2,3} | broadcast | bytes 30081024 | tf_op jit(solution)/shard_map/stack | solution.py:158
  98.6 6.8 all-to-all-start.1
  105.5 1.2 reduce-window.6
  107.6 1.4 fusion.47
  110.8 8.0 %convolution_convert_fusion.2 = bf16[512,512]{0,1:T(8,128)(2,1)S(1)} fusion(bf16[512,6144]{1,0:T(8,128)(2,1)} %all-gather.7.cloned.1.call-done, bf16[512,6144]{1,0:T(8,128)(2,1)} %param.14), kind=kOutput, calls=%fused_computation.44 | convolution fusion | flops 3221487616 | bytes 13107200 | tf_op jit(solution)/shard_map/td,fd->tf/dot_general | solution.py:86
  118.8 1.4 fusion.44
  120.3 536.1 %all-reduce = f32[64]{0:T(128)S(1)} all-reduce(f32[64]{0:T(128)S(1)} %bitcast_dynamic-update-slice_fusion), channel_id=2, replica_groups=mesh['seq'=16,'exp'=8] {'seq'}, use_global_device_ids=true, to_apply=%add | all-reduce | flops 64 | bytes 512
  657.4 2.7 fusion.64
  660.1 16.5 %while.28 = (s32[]{:T(128)}, f32[4,128,128]{2,1,0:T(8,128)S(1)}, s32[]{:T(128)}, f32[16,4]{1,0:T(8,128)S(1)}, f32[16,4,128,128]{3,2,1,0:T(8,128)}, /*index=5*/s32[]{:T(128)}, s32[]{:T(128)}) while((s32[]{:T(128)}, f32[4,128,128]{2,1,0:T(8,128)S(1)}, s32[]{:T(128)}, f32[16,4]{1,0:T(8,128)S(1)}, f32[16,4,128,128]{3,2,1,0:T(8,128)}, ...), condition=%wide.region_3.4_spmd.clone, body=%wide.region_2.3_spmd.clone.sunk | while | flops 262148 | bytes 786593 | solution.py:26
  660.1 1.1 fusion.86
  663.4 1.1 fusion.86
  664.5 1.1 fusion.86
  665.6 1.1 fusion.86
  667.8 1.1 fusion.86
  668.9 1.1 fusion.86
  670.1 1.1 fusion.86
  676.6 1.8 fusion.52
  678.5 3.5 fusion.23
  682.0 1.4 fusion.41
  683.4 2.1 copy.65
  685.5 6.0 fusion.29
  691.5 3.8 fusion.26
  695.3 4.8 rev.6
  700.1 16.5 %while.29 = (s32[]{:T(128)}, f32[4,128,128]{2,1,0:T(8,128)S(1)}, s32[]{:T(128)}, f32[16,4,128,128]{3,2,1,0:T(8,128)}, f32[16,4]{1,0:T(8,128)S(1)}, /*index=5*/s32[]{:T(128)}, s32[]{:T(128)}) while((s32[]{:T(128)}, f32[4,128,128]{2,1,0:T(8,128)S(1)}, s32[]{:T(128)}, f32[16,4,128,128]{3,2,1,0:T(8,128)}, f32[16,4]{1,0:T(8,128)S(1)}, ...), condition=%wide.region_5.6_spmd.clone, body=%wide.region_4.5_spmd.clone.sunk | while | flops 262148 | bytes 786593 | solution.py:26
  701.2 1.1 fusion.87
  702.3 1.1 fusion.87
  703.4 1.1 fusion.87
  704.5 1.1 fusion.87
  705.6 1.1 fusion.87
  706.7 1.1 fusion.87
  707.8 1.1 fusion.87
  708.9 1.1 fusion.87
  710.0 1.1 fusion.87
  711.1 1.1 fusion.87
  712.2 1.1 fusion.87
  713.3 1.1 fusion.87
  714.4 1.1 fusion.87
  715.5 1.1 fusion.87
  716.6 1.8 fusion.42
  719.4 1.9 fusion.43
  722.3 19.7 %copy.64 = bf16[2,16,72,6144]{3,2,1,0:T(8,128)(2,1)} copy(bf16[2,16,72,6144]{3,2,0,1:T(8,128)(2,1)} %bitcast.22) | data formatting | bytes 56623104 | tf_op jit(solution)/shard_map/reshape | solution.py:160
  742.0 20.9 %fusion.2 = bf16[2,288,6144]{2,1,0:T(8,128)(2,1)} fusion(bf16[2,288,1152]{2,1,0:T(8,128)(2,1)S(1)} %copy-done, bf16[2,1152,6144]{2,1,0:T(8,128)(2,1)} %bitcast.123), kind=kOutput, calls=%fused_computation.7 | convolution fusion | flops 8157265920 | bytes 36716544 | tf_op jit(solution)/shard_map/ehs,esd->ehd/dot_general | solution.py:161
  (100 shorter events, 18.4 us)
Async XLA Ops:
  7.2 734.8 %copy-start = (bf16[2,288,1152]{2,1,0:T(8,128)(2,1)S(1)}, bf16[2,288,1152]{2,1,0:T(8,128)(2,1)}, u32[]{:S(2)}) copy-start(bf16[2,288,1152]{2,1,0:T(8,128)(2,1)} %param.21) | copy-start | bytes 3981316
  7.2 103.6 %all-gather.7.cloned.1.call-start = ((), (), s32[]{:S(2)}) async-start(), calls=%async_computation.2 | async-start | bytes 7077888 | tf_op jit(solution)/shard_map/all_gather | solution.py:88
  98.6 6.9 copy-start.9
  98.6 8.7 %copy-start.5 = (bf16[512,512]{1,0:T(8,128)(2,1)S(1)}, bf16[512,512]{1,0:T(8,128)(2,1)}, u32[]{:S(2)}) copy-start(bf16[512,512]{1,0:T(8,128)(2,1)} %param.16) | copy-start | bytes 1572868
  98.6 9.0 %copy-start.3 = (bf16[512,512]{1,0:T(8,128)(2,1)S(1)}, bf16[512,512]{1,0:T(8,128)(2,1)}, u32[]{:S(2)}) copy-start(bf16[512,512]{1,0:T(8,128)(2,1)} %param.17) | copy-start | bytes 1572868
  98.6 10.7 %copy-start.6 = (bf16[512,512]{1,0:T(8,128)(2,1)S(1)}, bf16[512,512]{1,0:T(8,128)(2,1)}, u32[]{:S(2)}) copy-start(bf16[512,512]{1,0:T(8,128)(2,1)} %param.15) | copy-start | bytes 1572868
  98.6 10.9 %copy-start.10 = (u32[128]{0:T(128)S(1)}, u32[128]{0:T(128)}, u32[]{:S(2)}) copy-start(u32[128]{0:T(128)} %constant.76) | copy-start | bytes 1540
  98.6 623.7 %all-to-all-start.1 = ((bf16[16,2,72,6144]{3,2,1,0:T(8,128)(2,1)}), bf16[16,2,72,6144]{3,2,1,0:T(8,128)(2,1)}, u32[]{:S(2)}, u32[]{:S(2)}) async-start(bf16[16,2,72,6144]{3,2,1,0:T(8,128)(2,1)} %stack.5), calls=%async_computation.1 | async-start | bytes 56623104 | tf_op jit(solution)/shard_map/all_to_all | solution.py:159
  105.4 554.7 %all-gather.9.cloned.1.call-start = ((), (), s32[]{:S(2)}) async-start(), calls=%async_computation.3 | async-start | bytes 4456448 | tf_op jit(solution)/shard_map/all_gather | solution.py:14
  109.0 586.3 %all-gather.11.cloned.1.call-start = ((), (), s32[]{:S(2)}) async-start(), calls=%async_computation.4 | async-start | bytes 4456448 | tf_op jit(solution)/shard_map/all_gather | solution.py:14
  676.6 1.9 copy-start.7
  678.5 4.9 copy-start.1
  683.4 8.1 %copy-start.8 = (pred[512,512]{1,0:T(8,128)(4,1)S(1)}, pred[512,512]{1,0:T(8,128)(4,1)}, u32[]{:S(2)}) copy-start(pred[512,512]{1,0:T(8,128)(4,1)} %iota_compare_fusion) | copy-start | bytes 786436
  685.5 6.1 copy-start.2
  695.3 21.3 %copy-start.4 = (bf16[512,512]{1,0:T(8,128)(2,1)S(1)}, bf16[512,512]{1,0:T(8,128)(2,1)}, u32[]{:S(2)}) copy-start(bf16[512,512]{1,0:T(8,128)(2,1)} %param.17) | copy-start | bytes 1572868
Sparse Core Ops, SparseCore 0:
  9.7 77.4 all-gather.6
  109.1 459.1 all-gather.8
  570.5 105.1 all-gather.10
